TPU v7x, 32 devices: a whole 2x2x4 slice. The times are simulated.
32 devices in a mesh: dp: 8 (over z, x), tensor: 4 (over y, core).
Axes of the slice: x: 2, y: 2, z: 4, core: 2. Of those that a mesh axis runs over, the one named last changes fastest.
Arguments:
- tokens: bfloat16 [4096, 768], P(('dp', 'tensor')), may hold values from -20 to 20
- condition: bfloat16 [16, 768], P('dp'), may hold values from -4 to 4
- adaptive_weight: bfloat16 [768, 6, 768], P('dp', None, 'tensor'), may hold values from -0.21875 to 0.21875
- adaptive_bias: float32 [6, 768], P(None, 'tensor'), may hold values from -3 to 3
- entry_weight: bfloat16 [768, 3, 768], P('dp', None, 'tensor'), may hold values from -1 to 1
- entry_bias: float32 [2, 768], P(None, 'tensor'), may hold values from -3 to 3
- output_weight: bfloat16 [768, 768], P('tensor', 'dp'), may hold values from -0.875 to 0.875
- output_bias: float32 [768], replicated, may hold values from -3 to 3
- expand_weight: bfloat16 [768, 3072], P('dp', 'tensor'), may hold values from -0.21875 to 0.21875
- expand_bias: float32 [3072], P('tensor'), may hold values from -3 to 3
- reduce_weight: bfloat16 [3072, 768], P('tensor', 'dp'), may hold values from -0.109375 to 0.109375
- reduce_bias: float32 [768], replicated, may hold values from -3 to 3
- cotangent: bfloat16 [4096, 768], P(('dp', 'tensor')), may hold values from -6 to 6
Outputs:
- block_output: bfloat16 [4096, 768], P(('dp', 'tensor'))
- tokens_gradient: float32 [4096, 768], P(('dp', 'tensor'))
- condition_gradient: float32 [16, 768], P('dp')
- adaptive_gradient: float32 [768, 6, 768], P('dp', None, 'tensor')
- bias_adaptive: float32 [6, 768], P(None, 'tensor')
- entry_gradient: float32 [768, 3, 768], P('dp', None, 'tensor')
- bias_entry: float32 [2, 768], P(None, 'tensor')
- output_gradient: float32 [768, 768], P('tensor', 'dp')
- bias_output: float32 [768], replicated
- expand_gradient: float32 [768, 3072], P('dp', 'tensor')
- bias_expand: float32 [3072], P('tensor')
- reduce_gradient: float32 [3072, 768], P('tensor', 'dp')
- bias_reduce: float32 [768], replicated
All inputs are finite; a program needn't handle non-finite values.
Results may differ from a plain program's by a relative error of at most 0.015.
The roundings to bfloat16 on the way count: a program that leaves them out, or rounds other values in their place, can miss the bound.
Values may be sent and summed in bfloat16 or wider, within the bound.
A program may use at most 128 MiB of HBM per device.

v0:
```python
import jax
import jax.numpy as jnp
from jax import lax
from jax.sharding import PartitionSpec as P

HEAD_DIM = 64
LEN = 256
NORM_EPSILON = 1e-06
GELU_ROOT = 0.7978845608028654
GELU_CUBIC = 0.044715
HIGHEST_PRECISION = lax.Precision.HIGHEST


def norm_rows(values):
    center = values - jnp.mean(values, axis=-1, keepdims=True)
    inverse = lax.rsqrt(jnp.mean(center * center, axis=-1, keepdims=True) + NORM_EPSILON)
    return (center * inverse, inverse)


def norm_back(upstream, normed, inverse):
    return inverse * (
        upstream
        - jnp.mean(upstream, axis=-1, keepdims=True)
        - normed * jnp.mean(upstream * normed, axis=-1, keepdims=True)
    )


def gelu_pair(inputs):
    tangent = jnp.tanh(GELU_ROOT * (inputs + GELU_CUBIC * inputs * inputs * inputs))
    output = 0.5 * inputs * (1.0 + tangent)
    slope_value = 0.5 * (1.0 + tangent) + 0.5 * inputs * (1.0 - tangent * tangent) * GELU_ROOT * (
        1.0 + 3.0 * GELU_CUBIC * inputs * inputs
    )
    return (output, slope_value)


def contract_first(left, right):
    return lax.dot_general(
        left, right, (((0,), (0,)), ((), ())), preferred_element_type=jnp.float32
    )


def contract_last(left, right):
    return lax.dot_general(
        left, right, (((1,), (1,)), ((), ())), preferred_element_type=jnp.float32
    )


def gather_rows(values):
    return lax.all_gather(values, "tensor", axis=0, tiled=True)


def sum_rows(values):
    return lax.psum_scatter(
        values.astype(jnp.bfloat16), "tensor", scatter_dimension=0, tiled=True
    ).astype(jnp.float32)


def attend(query_rows, key_rows, value_rows):
    factor = query_rows.shape[-1] ** (-0.5)
    scores = (
        jnp.einsum("blhe,bmhe->bhlm", query_rows, key_rows, preferred_element_type=jnp.float32)
        * factor
    )
    row_top = jnp.max(scores, axis=-1, keepdims=True)
    log_total = row_top + jnp.log(jnp.sum(jnp.exp(scores - row_top), axis=-1, keepdims=True))
    weights = jnp.exp(scores - log_total).astype(jnp.bfloat16)
    attended = jnp.einsum(
        "bhlm,bmhe->blhe", weights, value_rows, preferred_element_type=jnp.float32
    )
    return (attended.astype(jnp.bfloat16), log_total)


def attend_back(query_rows, key_rows, value_rows, log_total, attended_grad):
    factor = query_rows.shape[-1] ** (-0.5)
    scores = (
        jnp.einsum("blhe,bmhe->bhlm", query_rows, key_rows, preferred_element_type=jnp.float32)
        * factor
    )
    probability = jnp.exp(scores - log_total)
    weights = probability.astype(jnp.bfloat16)
    value_grad = jnp.einsum(
        "bhlm,blhe->bmhe", weights, attended_grad, preferred_element_type=jnp.float32
    )
    weight_grad = jnp.einsum(
        "blhe,bmhe->bhlm", attended_grad, value_rows, preferred_element_type=jnp.float32
    )
    row_inner = jnp.sum(probability * weight_grad, axis=-1, keepdims=True)
    score_grad = (probability * (weight_grad - row_inner) * factor).astype(jnp.bfloat16)
    query_grad = jnp.einsum(
        "bhlm,bmhe->blhe", score_grad, key_rows, preferred_element_type=jnp.float32
    )
    key_grad = jnp.einsum(
        "bhlm,blhe->bmhe", score_grad, query_rows, preferred_element_type=jnp.float32
    )
    return (query_grad, key_grad, value_grad)


def body(
    tokens,
    condition,
    adaptive_weight,
    adaptive_bias,
    entry_weight,
    entry_bias,
    output_weight,
    output_bias,
    expand_weight,
    expand_bias,
    reduce_weight,
    reduce_bias,
    cotangent,
):
    tensor_index = lax.axis_index("tensor")
    tensor_count = lax.axis_size("tensor")
    row_count = tokens.shape[0]
    features = tokens.shape[1]
    seq_count = condition.shape[0]
    local_width = adaptive_bias.shape[1]
    local_hidden = expand_bias.shape[0]
    group_rows = row_count * tensor_count
    head_count = local_width // HEAD_DIM
    head_shape = (seq_count, LEN, head_count, HEAD_DIM)
    adaptive_full, entry_full, output_full, expand_full, reduce_full = (
        lax.all_gather(adaptive_weight, "dp", axis=0, tiled=True),
        lax.all_gather(entry_weight, "dp", axis=0, tiled=True),
        lax.all_gather(output_weight, "dp", axis=1, tiled=True),
        lax.all_gather(expand_weight, "dp", axis=0, tiled=True),
        lax.all_gather(reduce_weight, "dp", axis=1, tiled=True),
    )
    condition_float = condition.astype(jnp.float32)
    soft_condition = jax.nn.silu(condition_float).astype(jnp.bfloat16)
    modulation_local = (
        jnp.dot(
            soft_condition,
            adaptive_full.reshape(features, 6 * local_width),
            preferred_element_type=jnp.float32,
        ).reshape(seq_count, 6, local_width)
        + adaptive_bias[None]
    )
    modulation = lax.all_gather(modulation_local, "tensor", axis=2, tiled=True)
    seq_of_row = (tensor_index * row_count + jnp.arange(row_count, dtype=jnp.int32)) // LEN
    selector = (seq_of_row[:, None] == jnp.arange(seq_count, dtype=jnp.int32)[None, :]).astype(
        jnp.float32
    )
    per_row = jnp.dot(
        selector, modulation.reshape(seq_count, 6 * features), precision=HIGHEST_PRECISION
    ).reshape(row_count, 6, features)
    shift_one, scale_one, gate_one, shift_two, scale_two, gate_two = [
        per_row[:, column] for column in range(6)
    ]
    inputs = tokens.astype(jnp.float32)
    normed_one, inverse_one = norm_rows(inputs)
    attention_local = (normed_one * (1.0 + scale_one) + shift_one).astype(jnp.bfloat16)
    attention_input = gather_rows(attention_local)
    projected = jnp.dot(
        attention_input,
        entry_full.reshape(features, 3 * local_width),
        preferred_element_type=jnp.float32,
    ).reshape(group_rows, 3, local_width)
    query_rows = (projected[:, 0] + entry_bias[0]).astype(jnp.bfloat16).reshape(head_shape)
    key_rows = projected[:, 1].astype(jnp.bfloat16).reshape(head_shape)
    value_rows = (projected[:, 2] + entry_bias[1]).astype(jnp.bfloat16).reshape(head_shape)
    attended, log_total = attend(query_rows, key_rows, value_rows)
    attended = attended.reshape(group_rows, local_width)
    attention_branch = (
        sum_rows(jnp.dot(attended, output_full, preferred_element_type=jnp.float32)) + output_bias
    )
    middle = inputs + gate_one * attention_branch
    normed_two, inverse_two = norm_rows(middle)
    feed_local = (normed_two * (1.0 + scale_two) + shift_two).astype(jnp.bfloat16)
    feed_input = gather_rows(feed_local)
    hidden_pre = jnp.dot(feed_input, expand_full, preferred_element_type=jnp.float32) + expand_bias
    hidden_value, hidden_slope = gelu_pair(hidden_pre)
    hidden_rows = hidden_value.astype(jnp.bfloat16)
    feed_branch = (
        sum_rows(jnp.dot(hidden_rows, reduce_full, preferred_element_type=jnp.float32))
        + reduce_bias
    )
    block_output = (middle + gate_two * feed_branch).astype(jnp.bfloat16)
    adaptive_back, entry_back, output_back, expand_back, reduce_back = (
        lax.all_gather(adaptive_weight, "dp", axis=0, tiled=True),
        lax.all_gather(entry_weight, "dp", axis=0, tiled=True),
        lax.all_gather(output_weight, "dp", axis=1, tiled=True),
        lax.all_gather(expand_weight, "dp", axis=0, tiled=True),
        lax.all_gather(reduce_weight, "dp", axis=1, tiled=True),
    )
    upstream = cotangent.astype(jnp.float32)
    feed_grad = upstream * gate_two
    feed_gathered = gather_rows(feed_grad.astype(jnp.bfloat16))
    reduce_total = contract_first(hidden_rows, feed_gathered)
    hidden_grad = contract_last(feed_gathered, reduce_back) * hidden_slope
    hidden_round = hidden_grad.astype(jnp.bfloat16)
    expand_total = contract_first(feed_input, hidden_round)
    feed_input_grad = sum_rows(contract_last(hidden_round, expand_back))
    middle_grad = upstream + norm_back(feed_input_grad * (1.0 + scale_two), normed_two, inverse_two)
    attention_grad = middle_grad * gate_one
    attention_gathered = gather_rows(attention_grad.astype(jnp.bfloat16))
    output_total = contract_first(attended, attention_gathered)
    attended_grad = (
        contract_last(attention_gathered, output_back).astype(jnp.bfloat16).reshape(head_shape)
    )
    query_grad, key_grad, value_grad = attend_back(
        query_rows, key_rows, value_rows, log_total, attended_grad
    )
    query_grad = query_grad.reshape(group_rows, local_width)
    key_grad = key_grad.reshape(group_rows, local_width)
    value_grad = value_grad.reshape(group_rows, local_width)
    entry_round = (
        jnp.stack([query_grad, key_grad, value_grad], axis=1)
        .astype(jnp.bfloat16)
        .reshape(group_rows, 3 * local_width)
    )
    entry_total = contract_first(attention_input, entry_round).reshape(features, 3, local_width)
    input_grad = sum_rows(contract_last(entry_round, entry_back.reshape(features, 3 * local_width)))
    tokens_gradient = middle_grad + norm_back(
        input_grad * (1.0 + scale_one), normed_one, inverse_one
    )
    row_terms = jnp.stack(
        [
            input_grad,
            input_grad * normed_one,
            middle_grad * attention_branch,
            feed_input_grad,
            feed_input_grad * normed_two,
            upstream * feed_branch,
        ],
        axis=1,
    )
    per_sequence = lax.dot_general(
        selector,
        row_terms.reshape(row_count, 6 * features),
        (((0,), (0,)), ((), ())),
        precision=HIGHEST_PRECISION,
        preferred_element_type=jnp.float32,
    ).reshape(seq_count, 6, features)
    modulation_grad = lax.psum_scatter(
        per_sequence.astype(jnp.bfloat16), "tensor", scatter_dimension=2, tiled=True
    ).astype(jnp.float32)
    modulation_round = modulation_grad.astype(jnp.bfloat16).reshape(seq_count, 6 * local_width)
    adaptive_total = contract_first(soft_condition, modulation_round).reshape(
        features, 6, local_width
    )
    condition_partial = contract_last(
        modulation_round, adaptive_back.reshape(features, 6 * local_width)
    )
    condition_sum = lax.psum(condition_partial, "tensor")
    sigmoid_value = jax.nn.sigmoid(condition_float)
    condition_gradient = (
        condition_sum * sigmoid_value * (1.0 + condition_float * (1.0 - sigmoid_value))
    )
    adaptive_gradient, entry_gradient, output_gradient, expand_gradient, reduce_gradient = (
        lax.psum_scatter(adaptive_total, "dp", scatter_dimension=0, tiled=True),
        lax.psum_scatter(entry_total, "dp", scatter_dimension=0, tiled=True),
        lax.psum_scatter(output_total, "dp", scatter_dimension=1, tiled=True),
        lax.psum_scatter(expand_total, "dp", scatter_dimension=0, tiled=True),
        lax.psum_scatter(reduce_total, "dp", scatter_dimension=1, tiled=True),
    )
    width_start = tensor_index * local_width
    hidden_start = tensor_index * local_hidden
    adaptive_slot = lax.dynamic_update_slice_in_dim(
        jnp.zeros((6, features), jnp.float32), jnp.sum(modulation_grad, axis=0), width_start, 1
    )
    entry_slot = lax.dynamic_update_slice_in_dim(
        jnp.zeros((2, features), jnp.float32),
        jnp.stack([jnp.sum(query_grad, axis=0), jnp.sum(value_grad, axis=0)]),
        width_start,
        1,
    )
    expand_slot = lax.dynamic_update_slice_in_dim(
        jnp.zeros((local_hidden * tensor_count,), jnp.float32),
        jnp.sum(hidden_grad, axis=0),
        hidden_start,
        0,
    )
    adaptive_sums, entry_sums, output_sums, expand_sums, reduce_sums = lax.psum(
        (
            adaptive_slot,
            entry_slot,
            jnp.sum(attention_grad, axis=0),
            expand_slot,
            jnp.sum(feed_grad, axis=0),
        ),
        ("dp", "tensor"),
    )
    bias_adaptive = lax.dynamic_slice_in_dim(adaptive_sums, width_start, local_width, 1)
    bias_entry = lax.dynamic_slice_in_dim(entry_sums, width_start, local_width, 1)
    bias_expand = lax.dynamic_slice_in_dim(expand_sums, hidden_start, local_hidden, 0)
    return (
        block_output,
        tokens_gradient,
        condition_gradient,
        adaptive_gradient,
        bias_adaptive,
        entry_gradient,
        bias_entry,
        output_gradient,
        output_sums,
        expand_gradient,
        bias_expand,
        reduce_gradient,
        reduce_sums,
    )


def solution(mesh):
    in_specs = (
        P(("dp", "tensor"), None),
        P("dp", None),
        P("dp", None, "tensor"),
        P(None, "tensor"),
        P("dp", None, "tensor"),
        P(None, "tensor"),
        P("tensor", "dp"),
        P(),
        P("dp", "tensor"),
        P("tensor"),
        P("tensor", "dp"),
        P(),
        P(("dp", "tensor"), None),
    )
    out_specs = (
        P(("dp", "tensor"), None),
        P(("dp", "tensor"), None),
        P("dp", None),
        P("dp", None, "tensor"),
        P(None, "tensor"),
        P("dp", None, "tensor"),
        P(None, "tensor"),
        P("tensor", "dp"),
        P(),
        P("dp", "tensor"),
        P("tensor"),
        P("tensor", "dp"),
        P(),
    )
    return jax.shard_map(body, mesh=mesh, in_specs=in_specs, out_specs=out_specs, check_vma=False)
```

profile of v0, /device:TPU:0, one launch (start us, length us, event | category | flops | bytes accessed | tf_op | source)
XLA Modules:
  0.0 773.9 jit_solution(14435792287438220595)
XLA Ops:
  8.0 39.2 %all_gather.38 = bf16[768,3,192]{2,0,1:T(8,128)(2,1)S(1)} all-gather(bf16[96,3,192]{2,0,1:T(8,128)(2,1)} %param.17), channel_id=1, replica_groups=mesh['dp'=8,'tensor'=4] {'dp'}, dimensions={0}, use_global_device_ids=true | all-gather | bytes 995328 | tf_op jit(solution)/shard_map/all_gather | solution.py:126
  48.5 34.3 %all_gather.39 = bf16[192,768]{0,1:T(8,128)(2,1)} all-gather(bf16[192,96]{0,1:T(8,128)(2,1)S(1)} %copy.88), channel_id=1, replica_groups=mesh['dp'=8,'tensor'=4] {'dp'}, dimensions={1}, use_global_device_ids=true | all-gather | bytes 331776 | tf_op jit(solution)/shard_map/all_gather | solution.py:127
  86.4 8.9 %all_gather.36 = f32[2,6,768]{1,0,2:T(2,128)S(1)} all-gather(f32[2,6,192]{1,0,2:T(2,128)S(1)} %copy.80), channel_id=1, replica_groups=mesh['dp'=8,'tensor'=4] {'tensor'}, dimensions={2}, use_global_device_ids=true | all-gather | bytes 46080 | tf_op jit(solution)/shard_map/all_gather | solution.py:141
  97.1 8.7 %all_gather.37 = bf16[512,768]{1,0:T(8,128)(2,1)S(1)} all-gather(bf16[128,768]{1,0:T(8,128)(2,1)S(1)} %fusion.52), channel_id=1, replica_groups=mesh['dp'=8,'tensor'=4] {'tensor'}, dimensions={0}, use_global_device_ids=true | all-gather | bytes 983040 | tf_op jit(solution)/shard_map/all_gather | solution.py:50
  118.2 20.9 %reduce-scatter.15.cloned.1.call-done = bf16[128,768]{1,0:T(8,128)(2,1)} async-done(((bf16[512,768]{1,0:T(8,128)(2,1)}), bf16[128,768]{1,0:T(8,128)(2,1)}) %reduce-scatter.15.cloned.1.call-update) | async-done | bytes 196624 | tf_op jit(solution)/shard_map/reduce_scatter | solution.py:54
  140.6 8.5 %all_gather.40 = bf16[512,768]{1,0:T(8,128)(2,1)} all-gather(bf16[128,768]{1,0:T(8,128)(2,1)S(1)} %get-tuple-element.34), channel_id=1, replica_groups=mesh['dp'=8,'tensor'=4] {'tensor'}, dimensions={0}, use_global_device_ids=true | all-gather | bytes 983040 | tf_op jit(solution)/shard_map/all_gather | solution.py:50
  149.0 9.1 %all_gather.43 = bf16[512,768]{1,0:T(8,128)(2,1)} all-gather(bf16[128,768]{1,0:T(8,128)(2,1)S(1)} %get-tuple-element.33), channel_id=1, replica_groups=mesh['dp'=8,'tensor'=4] {'tensor'}, dimensions={0}, use_global_device_ids=true | all-gather | bytes 983040 | tf_op jit(solution)/shard_map/all_gather | solution.py:50
  158.2 24.2 %all-gather.6.cloned.1.call-done = bf16[768,768]{1,0:T(8,128)(2,1)} async-done(((bf16[96,768]{1,0:T(8,128)(2,1)}), bf16[768,768]{1,0:T(8,128)(2,1)}) %all-gather.6.cloned.1.call-update) | async-done | bytes 1179664 | tf_op jit(solution)/shard_map/all_gather | solution.py:128
  182.4 3.5 convolution_add_fusion
  185.9 38.4 %all-gather.8.cloned.1.call-done = bf16[768,768]{0,1:T(8,128)(2,1)} async-done(((bf16[768,96]{0,1:T(8,128)(2,1)}), bf16[768,768]{0,1:T(8,128)(2,1)}) %all-gather.8.cloned.1.call-update) | async-done | bytes 1179664 | tf_op jit(solution)/shard_map/all_gather | solution.py:129
  224.3 4.1 fusion.123
  231.1 3.8 convolution_convert_fusion.1
  234.9 18.2 %reduce-scatter.19.cloned.1.call-done = bf16[128,768]{1,0:T(8,128)(2,1)} async-done(((bf16[512,768]{1,0:T(8,128)(2,1)}), bf16[128,768]{1,0:T(8,128)(2,1)}) %reduce-scatter.19.cloned.1.call-update) | async-done | bytes 196624 | tf_op jit(solution)/shard_map/reduce_scatter | solution.py:54
  254.7 24.0 %reduce-scatter.17.cloned.1.call-done = bf16[128,768]{1,0:T(8,128)(2,1)} async-done(((bf16[512,768]{1,0:T(8,128)(2,1)}), bf16[128,768]{1,0:T(8,128)(2,1)}) %reduce-scatter.17.cloned.1.call-update) | async-done | bytes 196624 | tf_op jit(solution)/shard_map/reduce_scatter | solution.py:54
  280.7 8.2 %all_gather.44 = bf16[512,768]{1,0:T(8,128)(2,1)S(1)} all-gather(bf16[128,768]{1,0:T(8,128)(2,1)S(1)} %get-tuple-element.28), channel_id=1, replica_groups=mesh['dp'=8,'tensor'=4] {'tensor'}, dimensions={0}, use_global_device_ids=true | all-gather | bytes 983040 | tf_op jit(solution)/shard_map/all_gather | solution.py:50
  294.5 4.9 fusion.120
  299.4 4.4 fusion.23
  303.9 3.1 fusion.119
  315.1 3.3 bitcast_convert_fusion
  318.5 23.8 %reduce-scatter.21.cloned.1.call-done = bf16[128,768]{1,0:T(8,128)(2,1)} async-done(((bf16[512,768]{1,0:T(8,128)(2,1)}), bf16[128,768]{1,0:T(8,128)(2,1)}) %reduce-scatter.21.cloned.1.call-update) | async-done | bytes 196624 | tf_op jit(solution)/shard_map/reduce_scatter | solution.py:54
  353.9 3.4 fusion.27
  364.3 3.6 fusion.72
  369.1 3.8 fusion.115
  374.1 3.4 fusion.36
  377.7 5.0 reduce-scatter.31.cloned.1.call-done
  394.1 55.1 %reduce-scatter.33.cloned.1.call-done = f32[96,192]{1,0:T(8,128)} async-done(((f32[768,192]{1,0:T(8,128)}), f32[96,192]{1,0:T(8,128)}) %reduce-scatter.33.cloned.1.call-update) | async-done | bytes 73744
  454.8 42.1 %all-reduce = (f32[6,768]{1,0:T(8,128)S(1)}, f32[2,768]{1,0:T(2,128)S(1)}, f32[768]{0:T(1024)}, f32[3072]{0:T(1024)S(1)}, f32[768]{0:T(1024)}) all-reduce(f32[6,768]{1,0:T(8,128)S(1)} %dynamic_update_slice.9, f32[2,768]{1,0:T(2,128)} %dynamic_update_slice.10, ...), channel_id=1, replica_groups=mesh['dp'=8,'tensor'=4] {'dp','tensor'}, use_global_device_ids=true, to_apply=%region_19.20 | all-reduce | flops 10752 | bytes 86016 | tf_op jit(solution)/shard_map/psum | solution.py:276
  499.9 5.9 psum.42
  507.7 14.8 %reduce-scatter.27.cloned.1.call-done = f32[96,768]{1,0:T(8,128)} async-done(((f32[768,768]{1,0:T(8,128)}), f32[96,768]{1,0:T(8,128)}) %reduce-scatter.27.cloned.1.call-update) | async-done | bytes 294928 | tf_op jit(solution)/shard_map/reduce_scatter | solution.py:256
  522.6 72.9 %reduce-scatter.29.cloned.1.call-done = f32[768,96]{0,1:T(8,128)} async-done(((f32[768,768]{0,1:T(8,128)}), f32[768,96]{0,1:T(8,128)}) %reduce-scatter.29.cloned.1.call-update) | async-done | bytes 294928 | tf_op jit(solution)/shard_map/reduce_scatter | solution.py:257
  595.5 72.7 %reduce-scatter.25.cloned.1.call-done = f32[96,3,192]{2,0,1:T(8,128)} async-done(((f32[768,3,192]{2,0,1:T(8,128)}), f32[96,3,192]{2,0,1:T(8,128)}) %reduce-scatter.25.cloned.1.call-update) | async-done | bytes 221200 | tf_op jit(solution)/shard_map/reduce_scatter | solution.py:254
  668.2 99.1 %reduce-scatter.23.cloned.1.call-done = f32[96,6,192]{2,0,1:T(8,128)} async-done(((f32[768,6,192]{2,0,1:T(8,128)}), f32[96,6,192]{2,0,1:T(8,128)}) %reduce-scatter.23.cloned.1.call-update) | async-done | bytes 442384 | tf_op jit(solution)/shard_map/reduce_scatter | solution.py:253
  (202 shorter events, 84.1 us)
Async XLA Ops:
  7.2 75.7 %all-gather.4.cloned.1.call-start = ((), (), s32[]{:S(2)}) async-start(), calls=%async_computation.10 | async-start | bytes 2654208 | tf_op jit(solution)/shard_map/all_gather | solution.py:125
  7.9 131.2 %reduce-scatter.15.cloned.1.call-start = ((), (), s32[]{:S(2)}) async-start(), calls=%async_computation.11 | async-start | bytes 983040 | tf_op jit(solution)/shard_map/reduce_scatter | solution.py:54
  8.0 39.9 %copy-start.42 = (f32[2,192]{1,0:T(2,128)S(1)}, f32[2,192]{1,0:T(2,128)}, u32[]{:S(2)}) copy-start(f32[2,192]{1,0:T(2,128)} %param.18) | copy-start | bytes 4612
  8.0 40.1 %copy-start.27 = (bf16[192,96]{1,0:T(8,128)(2,1)S(1)}, bf16[192,96]{1,0:T(8,128)(2,1)}, u32[]{:S(2)}) copy-start(bf16[192,96]{1,0:T(8,128)(2,1)} %param.19) | copy-start | bytes 110596
  8.0 40.2 %copy-start.1 = (bf16[128,768]{1,0:T(8,128)(2,1)S(1)}, bf16[128,768]{1,0:T(8,128)(2,1)}, u32[]{:S(2)}) copy-start(bf16[128,768]{1,0:T(8,128)(2,1)} %param.13) | copy-start | bytes 589828
  47.2 35.6 %copy-start.6 = (bf16[768,3,192]{2,0,1:T(8,128)(2,1)}, bf16[768,3,192]{2,0,1:T(8,128)(2,1)S(1)}, u32[]{:S(2)}) copy-start(bf16[768,3,192]{2,0,1:T(8,128)(2,1)S(1)} %all_gather.38) | copy-start | bytes 2654212
  48.0 62.4 %copy-start.38 = (f32[3,64]{1,0:T(4,128)}, f32[3,64]{1,0:T(4,128)S(1)}, u32[]{:S(2)}) copy-start(f32[3,64]{1,0:T(4,128)S(1)} %add.200) | copy-start | bytes 2308
  48.2 47.6 %copy-start.43 = (s32[128]{0:T(128)}, s32[128]{0:T(128)S(1)}, u32[]{:S(2)}) copy-start(s32[128]{0:T(128)S(1)} %and_select_fusion) | copy-start | bytes 1540
  48.3 48.6 %copy-start.32 = (f32[128]{0:T(128)}, f32[128]{0:T(128)S(1)}, u32[]{:S(2)}) copy-start(f32[128]{0:T(128)S(1)} %broadcast_multiply_fusion.5) | copy-start | bytes 1540
  82.8 14.1 %copy-start.37 = (f32[128]{0:T(128)}, f32[128]{0:T(128)S(1)}, u32[]{:S(2)}) copy-start(f32[128]{0:T(128)S(1)} %add_rsqrt_fusion.1) | copy-start | bytes 1540
  114.5 24.6 %copy-start.29 = (f32[768]{0:T(1024)S(1)}, f32[768]{0:T(1024)}, u32[]{:S(2)}) copy-start(f32[768]{0:T(1024)} %param.20) | copy-start | bytes 9220
  116.8 23.5 %copy-start.14 = (bf16[128,768]{1,0:T(8,128)(2,1)S(1)}, bf16[128,768]{1,0:T(8,128)(2,1)}, u32[]{:S(2)}) copy-start(bf16[128,768]{1,0:T(8,128)(2,1)} %param.25) | copy-start | bytes 589828
  116.9 65.5 %all-gather.6.cloned.1.call-start = ((), (), s32[]{:S(2)}) async-start(), calls=%async_computation.12 | async-start | bytes 1327104 | tf_op jit(solution)/shard_map/all_gather | solution.py:128
  117.6 106.7 %all-gather.8.cloned.1.call-start = ((), (), s32[]{:S(2)}) async-start(), calls=%async_computation.13 | async-start | bytes 1327104 | tf_op jit(solution)/shard_map/all_gather | solution.py:129
  118.2 134.9 %reduce-scatter.19.cloned.1.call-start = ((), (), s32[]{:S(2)}) async-start(), calls=%async_computation.15 | async-start | bytes 983040 | tf_op jit(solution)/shard_map/reduce_scatter | solution.py:54
  231.0 22.1 %copy-start.35 = (f32[128]{0:T(128)S(1)}, f32[128]{0:T(128)}, u32[]{:S(2)}) copy-start(f32[128]{0:T(128)} %copy-done.34) | copy-start | bytes 1540
  231.0 22.1 %copy-start.41 = (f32[128]{0:T(128)S(1)}, f32[128]{0:T(128)}, u32[]{:S(2)}) copy-start(f32[128]{0:T(128)} %copy-done.40) | copy-start | bytes 1540
  231.0 47.7 %reduce-scatter.17.cloned.1.call-start = ((), (), s32[]{:S(2)}) async-start(), calls=%async_computation.14 | async-start | bytes 983040 | tf_op jit(solution)/shard_map/reduce_scatter | solution.py:54
  234.9 107.4 %reduce-scatter.21.cloned.1.call-start = ((), (), s32[]{:S(2)}) async-start(), calls=%async_computation.16 | async-start | bytes 983040 | tf_op jit(solution)/shard_map/reduce_scatter | solution.py:54
  278.7 11.1 %copy-start.9 = (bf16[192,768]{0,1:T(8,128)(2,1)S(1)}, bf16[192,768]{0,1:T(8,128)(2,1)}, u32[]{:S(2)}) copy-start(bf16[192,768]{0,1:T(8,128)(2,1)} %all_gather.39) | copy-start | bytes 884740
  280.7 65.3 %copy-start.4 = (f32[128,768]{1,0:T(8,128)}, f32[128,768]{1,0:T(8,128)S(1)}, u32[]{:S(2)}) copy-start(f32[128,768]{1,0:T(8,128)S(1)} %get-tuple-element.29) | copy-start | bytes 1179652
  315.1 29.0 %copy-start.33 = (f32[128]{0:T(128)S(1)}, f32[128]{0:T(128)}, u32[]{:S(2)}) copy-start(f32[128]{0:T(128)} %copy-done.32) | copy-start | bytes 1540
  318.4 27.5 %copy-start.30 = (f32[768]{0:T(1024)S(1)}, f32[768]{0:T(1024)}, u32[]{:S(2)}) copy-start(f32[768]{0:T(1024)} %param.20) | copy-start | bytes 9220
  318.4 29.3 %copy-start.13 = (bf16[128,768]{1,0:T(8,128)(2,1)S(1)}, bf16[128,768]{1,0:T(8,128)(2,1)}, u32[]{:S(2)}) copy-start(bf16[128,768]{1,0:T(8,128)(2,1)} %reduce-scatter.19.cloned.1.call-done) | copy-start | bytes 589828
  318.4 64.3 %reduce-scatter.31.cloned.1.call-start = ((), (), s32[]{:S(2)}) async-start(), calls=%async_computation.21 | async-start | bytes 245760
  362.8 86.4 %reduce-scatter.33.cloned.1.call-start = ((), (), s32[]{:S(2)}) async-start(), calls=%async_computation.22 | async-start | bytes 884736
  364.2 158.3 %reduce-scatter.27.cloned.1.call-start = ((), (), s32[]{:S(2)}) async-start(), calls=%async_computation.19 | async-start | bytes 2654208 | tf_op jit(solution)/shard_map/reduce_scatter | solution.py:256
  368.0 227.5 %reduce-scatter.29.cloned.1.call-start = ((), (), s32[]{:S(2)}) async-start(), calls=%async_computation.20 | async-start | bytes 2654208 | tf_op jit(solution)/shard_map/reduce_scatter | solution.py:257
  372.9 295.3 %reduce-scatter.25.cloned.1.call-start = ((), (), s32[]{:S(2)}) async-start(), calls=%async_computation.18 | async-start | bytes 2654208 | tf_op jit(solution)/shard_map/reduce_scatter | solution.py:254
  377.4 389.9 %reduce-scatter.23.cloned.1.call-start = ((), (), s32[]{:S(2)}) async-start(), calls=%async_computation.17 | async-start | bytes 5308416 | tf_op jit(solution)/shard_map/reduce_scatter | solution.py:253
  387.2 63.6 %copy-start.5 = (f32[128,768]{1,0:T(8,128)S(1)}, f32[128,768]{1,0:T(8,128)}, u32[]{:S(2)}) copy-start(f32[128,768]{1,0:T(8,128)} %copy-done.4) | copy-start | bytes 1179652
  387.2 63.6 %copy-start.10 = (bf16[128,768]{1,0:T(8,128)(2,1)S(1)}, bf16[128,768]{1,0:T(8,128)(2,1)}, u32[]{:S(2)}) copy-start(bf16[128,768]{1,0:T(8,128)(2,1)} %reduce-scatter.21.cloned.1.call-done) | copy-start | bytes 589828
  (27 other events, 98.5 us)
Sparse Core Ops, SparseCore 0:
  10.2 65.9 all-gather.3
  117.0 22.0 reduce-scatter.14
  141.3 41.0 all-gather.5
  184.4 39.8 all-gather.7
  231.1 21.9 reduce-scatter.18
  255.5 23.1 reduce-scatter.16
  318.5 23.7 reduce-scatter.20
  362.9 19.7 reduce-scatter.30
  386.0 63.1 reduce-scatter.32
  453.1 69.3 reduce-scatter.26
  526.6 68.8 reduce-scatter.28
  599.4 68.7 reduce-scatter.24
  672.4 94.8 reduce-scatter.22
where the time goes:
time: 775 us; the launch traced here: 774 us
  waiting for transfers between devices  471 us (61%)
  blocking collectives  165 us (21%)
  matrix products  59.7 us (8%)
  local copies, waits for them, and re-layouts  43.4 us (6%)
  other arithmetic  19.6 us (3%)
  between operations  14.4 us (2%)
    reduce_scatter x1, waiting for transfers between devices, body(): lax.psum_scatter(adaptive_total, 'dp', scatter_dimension=0, tiled=True)  99.1 us
    reduce_scatter x4, waiting for transfers between devices, sum_rows(): lax.psum_scatter(values.astype(jnp.bfloat16), 'tensor', scatter_dimension...  86.8 us
    reduce_scatter x1, waiting for transfers between devices, body(): lax.psum_scatter(reduce_total, 'dp', scatter_dimension=1, tiled=True)  72.9 us
    reduce_scatter x1, waiting for transfers between devices, body(): lax.psum_scatter(entry_total, 'dp', scatter_dimension=0, tiled=True)  72.7 us
    unnamed x15, waiting for transfers between devices  62.1 us
    psum x1, blocking collectives, body(): lax.psum((adaptive_slot, entry_slot, jnp.sum(attention_grad, axis=0), exp...  42.1 us
    all_gather x1, blocking collectives, body(): lax.all_gather(entry_weight, 'dp', axis=0, tiled=True)  39.2 us
    all_gather x1, waiting for transfers between devices, body(): lax.all_gather(reduce_weight, 'dp', axis=1, tiled=True)  38.4 us
  transfers between devices with their start and end apart: 13, of which 12 were waited for; matrix products, arithmetic and copies ran while one was open for 6% of the time, Pallas kernels for 0%

commit v1 on v0

--- a/solution.py
+++ b/solution.py
@@ -9,6 +9,27 @@
 GELU_ROOT = 0.7978845608028654
 GELU_CUBIC = 0.044715
 HIGHEST_PRECISION = lax.Precision.HIGHEST
+
+
+def joined_along(blocks, dim):
+    blocks = jnp.moveaxis(blocks, 0, dim)
+    shape = blocks.shape
+    return blocks.reshape(*shape[:dim], shape[dim] * shape[dim + 1], *shape[dim + 2 :])
+
+
+def grow_blocks(x, axis):
+    size, here = (lax.axis_size(axis), lax.axis_index(axis))
+    parts, bit = (x[None], 1)
+    while bit < size:
+        theirs = lax.ppermute(parts, axis, [(i, i ^ bit) for i in range(size)])
+        low = here & bit == 0
+        parts = jnp.concatenate([jnp.where(low, parts, theirs), jnp.where(low, theirs, parts)])
+        bit *= 2
+    return parts
+
+
+def doubled_up(x, axis, dim):
+    return joined_along(grow_blocks(x, axis), dim)
 
 
 def norm_rows(values):
@@ -123,7 +144,7 @@
     head_shape = (seq_count, LEN, head_count, HEAD_DIM)
     adaptive_full, entry_full, output_full, expand_full, reduce_full = (
         lax.all_gather(adaptive_weight, "dp", axis=0, tiled=True),
-        lax.all_gather(entry_weight, "dp", axis=0, tiled=True),
+        doubled_up(entry_weight, "dp", 0),
         lax.all_gather(output_weight, "dp", axis=1, tiled=True),
         lax.all_gather(expand_weight, "dp", axis=0, tiled=True),
         lax.all_gather(reduce_weight, "dp", axis=1, tiled=True),

time: 775 us -> 787 us (1.015)
  waiting for transfers between devices: 471 us -> 445 us
  blocking collectives: 165 us -> 189 us
  starting transfers between devices: 0.75 us -> 10.6 us
    reduce_scatter x4, waiting for transfers between devices: 86.8 us -> 48.6 us  [sum_rows(): lax.psum_scatter(values.astype(jnp.bfloat16), 'tensor', scatter_dimension...]
    all_gather x1, blocking collectives: 34.3 us -> 61.9 us  [body(): lax.all_gather(output_weight, 'dp', axis=1, tiled=True)]
    ppermute x0 -> x3, waiting for transfers between devices: none -> 11.9 us  [grow_blocks(): theirs = lax.ppermute(parts, axis, [(i, i ^ bit) for i in range(size)])]
    ppermute x0 -> x3, starting transfers between devices: none -> 9.87 us  [grow_blocks(): theirs = lax.ppermute(parts, axis, [(i, i ^ bit) for i in range(size)])]
  transfers between devices with their start and end apart: 13 -> 16, of which waited for: 12 -> 13; matrix products, arithmetic and copies ran while one was open for 6% -> 6% of each run, Pallas kernels for 0% -> 0%
where the time goes in v1:
time: 787 us; the launch traced here: 785 us
  waiting for transfers between devices  445 us (57%)
  blocking collectives  189 us (24%)
  matrix products  59.7 us (8%)
  local copies, waits for them, and re-layouts  45.1 us (6%)
  other arithmetic  22 us (3%)
  between operations  14.5 us (2%)
  starting transfers between devices  10.6 us (1%)
    reduce_scatter x1, waiting for transfers between devices, body(): lax.psum_scatter(adaptive_total, 'dp', scatter_dimension=0, tiled=True)  99.1 us
    reduce_scatter x1, waiting for transfers between devices, body(): lax.psum_scatter(reduce_total, 'dp', scatter_dimension=1, tiled=True)  72.9 us
    reduce_scatter x1, waiting for transfers between devices, body(): lax.psum_scatter(entry_total, 'dp', scatter_dimension=0, tiled=True)  72.8 us
    unnamed x15, waiting for transfers between devices  62.3 us
    all_gather x1, blocking collectives, body(): lax.all_gather(output_weight, 'dp', axis=1, tiled=True)  61.9 us
    reduce_scatter x4, waiting for transfers between devices, sum_rows(): lax.psum_scatter(values.astype(jnp.bfloat16), 'tensor', scatter_dimension...  48.6 us
    psum x1, blocking collectives, body(): lax.psum((adaptive_slot, entry_slot, jnp.sum(attention_grad, axis=0), exp...  42.3 us
    all_gather x1, waiting for transfers between devices, body(): lax.all_gather(reduce_weight, 'dp', axis=1, tiled=True)  38.4 us
  transfers between devices with their start and end apart: 16, of which 13 were waited for; matrix products, arithmetic and copies ran while one was open for 6% of the time, Pallas kernels for 0%

profile of v1, /device:TPU:0, one launch (start us, length us, event | category | flops | bytes accessed | tf_op | source)
XLA Modules:
  0.0 785.4 jit_solution(12139653998249942037)
XLA Ops:
  18.5 8.9 %collective-permute-done.1 = bf16[2,96,3,192]{3,1,2,0:T(8,128)(2,1)S(1)} collective-permute-done((bf16[2,96,3,192]{3,1,2,0:T(8,128)(2,1)S(1)}, bf16[2,96,3,192]{3,1,2,0:T(8,128)(2,1)S(1)}, u32[]{:S(2)}, u32[]{:S(2)}) %collective-permute-start.1) | collective-permute-done | bytes 221216 | tf_op jit(solution)/shard_map/ppermute | solution.py:24
  27.5 5.0 collective-permute-start.2
  32.5 61.9 %all_gather.37 = bf16[192,768]{0,1:T(8,128)(2,1)} all-gather(bf16[192,96]{0,1:T(8,128)(2,1)S(1)} %copy.88), channel_id=1, replica_groups=mesh['dp'=8,'tensor'=4] {'dp'}, dimensions={1}, use_global_device_ids=true | all-gather | bytes 331776 | tf_op jit(solution)/shard_map/all_gather | solution.py:148
  100.8 8.7 %all_gather.35 = f32[2,6,768]{1,0,2:T(2,128)S(1)} all-gather(f32[2,6,192]{1,0,2:T(2,128)S(1)} %copy.80), channel_id=1, replica_groups=mesh['dp'=8,'tensor'=4] {'tensor'}, dimensions={2}, use_global_device_ids=true | all-gather | bytes 46080 | tf_op jit(solution)/shard_map/all_gather | solution.py:162
  111.3 8.7 %all_gather.36 = bf16[512,768]{1,0:T(8,128)(2,1)S(1)} all-gather(bf16[128,768]{1,0:T(8,128)(2,1)S(1)} %fusion.51), channel_id=1, replica_groups=mesh['dp'=8,'tensor'=4] {'tensor'}, dimensions={0}, use_global_device_ids=true | all-gather | bytes 983040 | tf_op jit(solution)/shard_map/all_gather | solution.py:71
  132.3 18.3 %reduce-scatter.15.cloned.1.call-done = bf16[128,768]{1,0:T(8,128)(2,1)} async-done(((bf16[512,768]{1,0:T(8,128)(2,1)}), bf16[128,768]{1,0:T(8,128)(2,1)}) %reduce-scatter.15.cloned.1.call-update) | async-done | bytes 196624 | tf_op jit(solution)/shard_map/reduce_scatter | solution.py:75
  152.1 8.5 %all_gather.38 = bf16[512,768]{1,0:T(8,128)(2,1)} all-gather(bf16[128,768]{1,0:T(8,128)(2,1)S(1)} %get-tuple-element.34), channel_id=1, replica_groups=mesh['dp'=8,'tensor'=4] {'tensor'}, dimensions={0}, use_global_device_ids=true | all-gather | bytes 983040 | tf_op jit(solution)/shard_map/all_gather | solution.py:71
  160.6 9.3 %all_gather.41 = bf16[512,768]{1,0:T(8,128)(2,1)} all-gather(bf16[128,768]{1,0:T(8,128)(2,1)S(1)} %get-tuple-element.33), channel_id=1, replica_groups=mesh['dp'=8,'tensor'=4] {'tensor'}, dimensions={0}, use_global_device_ids=true | all-gather | bytes 983040 | tf_op jit(solution)/shard_map/all_gather | solution.py:71
  169.9 24.0 %all-gather.6.cloned.1.call-done = bf16[768,768]{1,0:T(8,128)(2,1)} async-done(((bf16[96,768]{1,0:T(8,128)(2,1)}), bf16[768,768]{1,0:T(8,128)(2,1)}) %all-gather.6.cloned.1.call-update) | async-done | bytes 1179664 | tf_op jit(solution)/shard_map/all_gather | solution.py:149
  193.9 3.5 convolution_add_fusion
  197.4 38.4 %all-gather.8.cloned.1.call-done = bf16[768,768]{0,1:T(8,128)(2,1)} async-done(((bf16[768,96]{0,1:T(8,128)(2,1)}), bf16[768,768]{0,1:T(8,128)(2,1)}) %all-gather.8.cloned.1.call-update) | async-done | bytes 1179664 | tf_op jit(solution)/shard_map/all_gather | solution.py:150
  235.8 4.1 fusion.122
  242.6 3.8 convolution_convert_fusion.1
  246.5 35.4 %all_gather.43 = bf16[768,3,192]{2,0,1:T(8,128)(2,1)} all-gather(bf16[96,3,192]{2,0,1:T(8,128)(2,1)S(1)} %copy-done.23), channel_id=1, replica_groups=mesh['dp'=8,'tensor'=4] {'dp'}, dimensions={0}, use_global_device_ids=true | all-gather | bytes 995328 | tf_op jit(solution)/shard_map/all_gather | solution.py:204
  283.6 6.7 reduce-scatter.17.cloned.1.call-done
  292.2 8.0 %all_gather.42 = bf16[512,768]{1,0:T(8,128)(2,1)S(1)} all-gather(bf16[128,768]{1,0:T(8,128)(2,1)S(1)} %get-tuple-element.28), channel_id=1, replica_groups=mesh['dp'=8,'tensor'=4] {'tensor'}, dimensions={0}, use_global_device_ids=true | all-gather | bytes 983040 | tf_op jit(solution)/shard_map/all_gather | solution.py:71
  305.8 5.0 fusion.119
  310.8 4.4 fusion.23
  326.4 3.4 bitcast_convert_fusion
  330.1 23.6 %reduce-scatter.21.cloned.1.call-done = bf16[128,768]{1,0:T(8,128)(2,1)} async-done(((bf16[512,768]{1,0:T(8,128)(2,1)}), bf16[128,768]{1,0:T(8,128)(2,1)}) %reduce-scatter.21.cloned.1.call-update) | async-done | bytes 196624 | tf_op jit(solution)/shard_map/reduce_scatter | solution.py:75
  365.3 3.4 fusion.27
  375.7 3.7 fusion.71
  380.5 3.8 fusion.114
  385.5 3.3 fusion.34
  388.9 5.2 reduce-scatter.31.cloned.1.call-done
  405.6 55.0 %reduce-scatter.33.cloned.1.call-done = f32[96,192]{1,0:T(8,128)} async-done(((f32[768,192]{1,0:T(8,128)}), f32[96,192]{1,0:T(8,128)}) %reduce-scatter.33.cloned.1.call-update) | async-done | bytes 73744
  466.1 42.3 %all-reduce = (f32[6,768]{1,0:T(8,128)S(1)}, f32[2,768]{1,0:T(2,128)S(1)}, f32[768]{0:T(1024)}, f32[3072]{0:T(1024)S(1)}, f32[768]{0:T(1024)}) all-reduce(f32[6,768]{1,0:T(8,128)S(1)} %dynamic_update_slice.9, f32[2,768]{1,0:T(2,128)} %dynamic_update_slice.10, ...), channel_id=1, replica_groups=mesh['dp'=8,'tensor'=4] {'dp','tensor'}, use_global_device_ids=true, to_apply=%region_19.20 | all-reduce | flops 10752 | bytes 86016 | tf_op jit(solution)/shard_map/psum | solution.py:297
  511.4 5.9 psum.42
  519.3 14.8 %reduce-scatter.27.cloned.1.call-done = f32[96,768]{1,0:T(8,128)} async-done(((f32[768,768]{1,0:T(8,128)}), f32[96,768]{1,0:T(8,128)}) %reduce-scatter.27.cloned.1.call-update) | async-done | bytes 294928 | tf_op jit(solution)/shard_map/reduce_scatter | solution.py:277
  534.0 72.9 %reduce-scatter.29.cloned.1.call-done = f32[768,96]{0,1:T(8,128)} async-done(((f32[768,768]{0,1:T(8,128)}), f32[768,96]{0,1:T(8,128)}) %reduce-scatter.29.cloned.1.call-update) | async-done | bytes 294928 | tf_op jit(solution)/shard_map/reduce_scatter | solution.py:278
  606.9 72.8 %reduce-scatter.25.cloned.1.call-done = f32[96,3,192]{2,0,1:T(8,128)} async-done(((f32[768,3,192]{2,0,1:T(8,128)}), f32[96,3,192]{2,0,1:T(8,128)}) %reduce-scatter.25.cloned.1.call-update) | async-done | bytes 221200 | tf_op jit(solution)/shard_map/reduce_scatter | solution.py:275
  679.7 99.1 %reduce-scatter.23.cloned.1.call-done = f32[96,6,192]{2,0,1:T(8,128)} async-done(((f32[768,6,192]{2,0,1:T(8,128)}), f32[96,6,192]{2,0,1:T(8,128)}) %reduce-scatter.23.cloned.1.call-update) | async-done | bytes 442384 | tf_op jit(solution)/shard_map/reduce_scatter | solution.py:274
  (215 shorter events, 99.0 us)
Async XLA Ops:
  7.2 11.1 %copy-start.1 = (bf16[128,768]{1,0:T(8,128)(2,1)S(1)}, bf16[128,768]{1,0:T(8,128)(2,1)}, u32[]{:S(2)}) copy-start(bf16[128,768]{1,0:T(8,128)(2,1)} %param.13) | copy-start | bytes 589828
  7.2 11.0 %copy-start.27 = (bf16[192,96]{1,0:T(8,128)(2,1)S(1)}, bf16[192,96]{1,0:T(8,128)(2,1)}, u32[]{:S(2)}) copy-start(bf16[192,96]{1,0:T(8,128)(2,1)} %param.19) | copy-start | bytes 110596
  7.2 90.0 %all-gather.4.cloned.1.call-start = ((), (), s32[]{:S(2)}) async-start(), calls=%async_computation.10 | async-start | bytes 2654208 | tf_op jit(solution)/shard_map/all_gather | solution.py:146
  7.9 142.6 %reduce-scatter.15.cloned.1.call-start = ((), (), s32[]{:S(2)}) async-start(), calls=%async_computation.11 | async-start | bytes 983040 | tf_op jit(solution)/shard_map/reduce_scatter | solution.py:75
  8.0 7.1 collective-permute-start
  12.1 99.0 %copy-start.32 = (f32[128]{0:T(128)}, f32[128]{0:T(128)S(1)}, u32[]{:S(2)}) copy-start(f32[128]{0:T(128)S(1)} %broadcast_multiply_fusion.5) | copy-start | bytes 1540
  16.1 11.3 %collective-permute-start.1 = (bf16[2,96,3,192]{3,1,2,0:T(8,128)(2,1)S(1)}, bf16[2,96,3,192]{3,1,2,0:T(8,128)(2,1)S(1)}, u32[]{:S(2)}, u32[]{:S(2)}) collective-permute-start(bf16[2,96,3,192]{3,1,2,0:T(8,128)(2,1)S(1)} %pad_maximum_fusion.2), channel_id=1, source_target_pairs={{0,8},{4,12},{8,0},{12,4},{16,24},{20,28},{24,16},{28,20},{1,9},{5... | collective-permute-start | bytes 663560 | tf_op jit(solution)/shard_map/ppermute | solution.py:24
  18.1 106.4 %copy-start.38 = (f32[3,64]{1,0:T(4,128)}, f32[3,64]{1,0:T(4,128)S(1)}, u32[]{:S(2)}) copy-start(f32[3,64]{1,0:T(4,128)S(1)} %add.200) | copy-start | bytes 2308
  27.5 66.9 %collective-permute-start.2 = (bf16[4,96,3,192]{3,1,2,0:T(8,128)(2,1)S(1)}, bf16[4,96,3,192]{3,1,2,0:T(8,128)(2,1)S(1)}, u32[]{:S(2)}, u32[]{:S(2)}) collective-permute-start(bf16[4,96,3,192]{3,1,2,0:T(8,128)(2,1)S(1)} %pad_maximum_fusion.1), channel_id=1, source_target_pairs={{0,16},{4,20},{8,24},{12,28},{16,0},{20,4},{24,8},{28,12},{1,17},{... | collective-permute-start | bytes 1327112 | tf_op jit(solution)/shard_map/ppermute | solution.py:24
  32.5 77.4 %copy-start.43 = (s32[128]{0:T(128)}, s32[128]{0:T(128)S(1)}, u32[]{:S(2)}) copy-start(s32[128]{0:T(128)S(1)} %and_select_fusion) | copy-start | bytes 1540
  94.4 16.6 %copy-start.37 = (f32[128]{0:T(128)}, f32[128]{0:T(128)S(1)}, u32[]{:S(2)}) copy-start(f32[128]{0:T(128)S(1)} %add_rsqrt_fusion.1) | copy-start | bytes 1540
  128.6 22.0 %copy-start.29 = (f32[768]{0:T(1024)S(1)}, f32[768]{0:T(1024)}, u32[]{:S(2)}) copy-start(f32[768]{0:T(1024)} %param.20) | copy-start | bytes 9220
  130.9 21.0 %copy-start.13 = (bf16[128,768]{1,0:T(8,128)(2,1)S(1)}, bf16[128,768]{1,0:T(8,128)(2,1)}, u32[]{:S(2)}) copy-start(bf16[128,768]{1,0:T(8,128)(2,1)} %param.25) | copy-start | bytes 589828
  130.9 63.0 %all-gather.6.cloned.1.call-start = ((), (), s32[]{:S(2)}) async-start(), calls=%async_computation.12 | async-start | bytes 1327104 | tf_op jit(solution)/shard_map/all_gather | solution.py:149
  131.6 104.2 %all-gather.8.cloned.1.call-start = ((), (), s32[]{:S(2)}) async-start(), calls=%async_computation.13 | async-start | bytes 1327104 | tf_op jit(solution)/shard_map/all_gather | solution.py:150
  132.2 149.7 %reduce-scatter.19.cloned.1.call-start = ((), (), s32[]{:S(2)}) async-start(), calls=%async_computation.15 | async-start | bytes 983040 | tf_op jit(solution)/shard_map/reduce_scatter | solution.py:75
  242.5 47.7 %reduce-scatter.17.cloned.1.call-start = ((), (), s32[]{:S(2)}) async-start(), calls=%async_computation.14 | async-start | bytes 983040 | tf_op jit(solution)/shard_map/reduce_scatter | solution.py:75
  246.4 35.5 %copy-start.35 = (f32[128]{0:T(128)S(1)}, f32[128]{0:T(128)}, u32[]{:S(2)}) copy-start(f32[128]{0:T(128)} %copy-done.34) | copy-start | bytes 1540
  246.4 35.5 %copy-start.41 = (f32[128]{0:T(128)S(1)}, f32[128]{0:T(128)}, u32[]{:S(2)}) copy-start(f32[128]{0:T(128)} %copy-done.40) | copy-start | bytes 1540
  246.4 107.3 %reduce-scatter.21.cloned.1.call-start = ((), (), s32[]{:S(2)}) async-start(), calls=%async_computation.16 | async-start | bytes 983040 | tf_op jit(solution)/shard_map/reduce_scatter | solution.py:75
  292.2 65.1 %copy-start.4 = (f32[128,768]{1,0:T(8,128)}, f32[128,768]{1,0:T(8,128)S(1)}, u32[]{:S(2)}) copy-start(f32[128,768]{1,0:T(8,128)S(1)} %get-tuple-element.29) | copy-start | bytes 1179652
  326.4 29.0 %copy-start.33 = (f32[128]{0:T(128)S(1)}, f32[128]{0:T(128)}, u32[]{:S(2)}) copy-start(f32[128]{0:T(128)} %copy-done.32) | copy-start | bytes 1540
  329.8 27.6 %copy-start.30 = (f32[768]{0:T(1024)S(1)}, f32[768]{0:T(1024)}, u32[]{:S(2)}) copy-start(f32[768]{0:T(1024)} %param.20) | copy-start | bytes 9220
  329.8 29.3 %copy-start.12 = (bf16[128,768]{1,0:T(8,128)(2,1)S(1)}, bf16[128,768]{1,0:T(8,128)(2,1)}, u32[]{:S(2)}) copy-start(bf16[128,768]{1,0:T(8,128)(2,1)} %reduce-scatter.19.cloned.1.call-done) | copy-start | bytes 589828
  329.8 64.3 %reduce-scatter.31.cloned.1.call-start = ((), (), s32[]{:S(2)}) async-start(), calls=%async_computation.21 | async-start | bytes 245760
  374.2 86.4 %reduce-scatter.33.cloned.1.call-start = ((), (), s32[]{:S(2)}) async-start(), calls=%async_computation.22 | async-start | bytes 884736
  375.7 158.4 %reduce-scatter.27.cloned.1.call-start = ((), (), s32[]{:S(2)}) async-start(), calls=%async_computation.19 | async-start | bytes 2654208 | tf_op jit(solution)/shard_map/reduce_scatter | solution.py:277
  379.4 227.5 %reduce-scatter.29.cloned.1.call-start = ((), (), s32[]{:S(2)}) async-start(), calls=%async_computation.20 | async-start | bytes 2654208 | tf_op jit(solution)/shard_map/reduce_scatter | solution.py:278
  384.4 295.4 %reduce-scatter.25.cloned.1.call-start = ((), (), s32[]{:S(2)}) async-start(), calls=%async_computation.18 | async-start | bytes 2654208 | tf_op jit(solution)/shard_map/reduce_scatter | solution.py:275
  388.8 390.0 %reduce-scatter.23.cloned.1.call-start = ((), (), s32[]{:S(2)}) async-start(), calls=%async_computation.17 | async-start | bytes 5308416 | tf_op jit(solution)/shard_map/reduce_scatter | solution.py:274
  398.6 63.6 %copy-start.5 = (f32[128,768]{1,0:T(8,128)S(1)}, f32[128,768]{1,0:T(8,128)}, u32[]{:S(2)}) copy-start(f32[128,768]{1,0:T(8,128)} %copy-done.4) | copy-start | bytes 1179652
  398.6 63.6 %copy-start.9 = (bf16[128,768]{1,0:T(8,128)(2,1)S(1)}, bf16[128,768]{1,0:T(8,128)(2,1)}, u32[]{:S(2)}) copy-start(bf16[128,768]{1,0:T(8,128)(2,1)} %reduce-scatter.21.cloned.1.call-done) | copy-start | bytes 589828
  (30 other events, 124.0 us)
Sparse Core Ops, SparseCore 0:
  10.2 72.7 all-gather.3
  131.0 19.5 reduce-scatter.14
  152.8 41.0 all-gather.5
  196.0 39.8 all-gather.7
  242.7 21.8 reduce-scatter.18
  267.0 23.2 reduce-scatter.16
  329.9 23.7 reduce-scatter.20
  374.3 19.7 reduce-scatter.30
  397.4 63.1 reduce-scatter.32
  464.5 69.4 reduce-scatter.26
  538.1 68.7 reduce-scatter.28
  610.8 68.8 reduce-scatter.24
  683.9 94.8 reduce-scatter.22
